TPU v7x, 128 devices: a whole 4x4x4 slice. The times are simulated.
128 devices in a mesh: cent: 4 (over y), rows: 32 (over z, x, core).
Axes of the slice: x: 4, y: 4, z: 4, core: 2. Of those that a mesh axis runs over, the one named last changes fastest.
Arguments:
- embeddings: bfloat16 [32768, 2048], P(('cent', 'rows')), may hold values from -6 to 6
- centroids: bfloat16 [16384, 2048], P(('cent', 'rows')), may hold values from -0.125 to 0.125
- cluster: int32 [32768, 1], P(('cent', 'rows')), may hold values from 0 to 127; in each aligned block of 256 rows (0 to 255, 256 to 511, ...) at most 4 rows name the same one
- noise_salt: int32 [1], replicated, may hold values from 0 to 1048575
Outputs:
- perturbed_max: float32 [32768], P(('cent', 'rows'))
- dedup_score: float32 [32768], P(('cent', 'rows'))
- new_centroids: float32 [128, 2048], P(('cent', 'rows'))
Inputs may be any that keep to these rules, and one draw needn't show every extreme that they name: In every aligned block of 256 rows (the rows of one device) no cluster is named by more than 4 rows, and in some block some cluster by exactly 4; every cluster is named by some row.
All inputs are finite; a program needn't handle non-finite values.
Results may differ from a plain program's by a relative error of at most 0.0003.
Values may be sent and summed in bfloat16 or wider, within the bound.
A program may use at most 128 MiB of HBM per device.

v0:
```python
import math
import jax
import jax.numpy as jnp
from jax import lax
from jax.sharding import PartitionSpec as P

inverse_temp = 3.0
epsilon = 1e-06


def logical_shift(word, amount):
    return lax.shift_right_logical(word, jnp.full(word.shape, amount, jnp.int32))


def gumbel_noise(row_ids, cent_ids, salt_word):
    mixed = row_ids * 1103515245 + cent_ids * 739982445 + salt_word
    mixed = mixed ^ logical_shift(mixed, 16)
    mixed = mixed * 2146121005
    mixed = mixed ^ logical_shift(mixed, 15)
    mixed = mixed * 1759714725
    mixed = mixed ^ logical_shift(mixed, 16)
    low_bits = mixed & 8388607
    uniform = (low_bits.astype(jnp.float32) + 0.5) * (1.0 / 8388608.0)
    return -jnp.log(-jnp.log(uniform))


def cluster_stats(members, valid):
    feature_dim = members.shape[1]
    widened = members.astype(jnp.float32)
    scale = lax.rsqrt(jnp.mean(widened * widened, axis=1) + epsilon)
    gram = lax.dot_general(
        members, members, (((1,), (1,)), ((), ())), preferred_element_type=jnp.float32
    )
    similar = gram * scale[:, None] * scale[None, :] * (1.0 / math.sqrt(feature_dim))
    order = jnp.arange(members.shape[0], dtype=jnp.int32)
    usable = valid[None, :] & (order[:, None] != order[None, :])
    highest = jnp.max(jnp.where(usable, similar, -1e30), axis=1)
    scores = jnp.where(jnp.any(usable, axis=1), highest, 0.0)
    total = jnp.sum(jnp.where(valid[:, None], widened, 0.0), axis=0)
    center = total * lax.rsqrt(jnp.mean(total * total) + epsilon)
    return (scores, center)


def shards(embeddings, centroids, cluster, noise_salt):
    rows_dev, feature_dim = embeddings.shape
    cent_dev = centroids.shape[0]
    cent_count = lax.axis_size("cent")
    rows_count = lax.axis_size("rows")
    devices = cent_count * rows_count
    capacity = max(2, 2 * rows_dev // devices)
    cent_index = lax.axis_index("cent")
    rows_index = lax.axis_index("rows")
    salt_word = noise_salt[0]
    group = lax.all_gather(embeddings, "cent", axis=0, tiled=True)
    position = jnp.arange(cent_count * rows_dev, dtype=jnp.int32)
    group_ids = (position // rows_dev * rows_count + rows_index) * rows_dev + position % rows_dev
    panel_base = cent_index * (rows_count * cent_dev)
    initial = jnp.full((cent_count * rows_dev,), -1e30, jnp.float32)
    piece = lax.all_gather(centroids, "rows", axis=0, tiled=True)
    piece_rows = piece.shape[0]
    block = math.gcd(piece_rows, 512)
    tiles = piece.reshape(piece_rows // block, block, feature_dim)
    offsets = jnp.arange(piece_rows // block, dtype=jnp.int32) * block

    def step(carry, item):
        tile, offset = item
        scores = lax.dot_general(
            group, tile, (((1,), (1,)), ((), ())), preferred_element_type=jnp.float32
        )
        cent_ids = panel_base + offset + jnp.arange(block, dtype=jnp.int32)
        perturbed = inverse_temp * scores + gumbel_noise(
            group_ids[:, None], cent_ids[None, :], salt_word
        )
        return (jnp.maximum(carry, jnp.max(perturbed, axis=1)), None)

    result, unused = lax.scan(step, initial, (tiles, offsets))
    merged = lax.pmax(result, "cent")
    perturbed_max = lax.dynamic_slice_in_dim(merged, cent_index * rows_dev, rows_dev)
    assigned = cluster[:, 0]
    order = jnp.arange(rows_dev, dtype=jnp.int32)
    same = (assigned[:, None] == assigned[None, :]) & (order[None, :] < order[:, None])
    rank = jnp.sum(same.astype(jnp.int32), axis=1)
    slot = assigned * capacity + rank
    outgoing = jnp.zeros((devices * capacity, feature_dim), jnp.bfloat16).at[slot].set(embeddings)
    present = (
        jnp.zeros((devices * capacity,), jnp.bfloat16)
        .at[slot]
        .set(jnp.ones((rows_dev,), jnp.bfloat16))
    )
    received, arrived = (
        lax.all_to_all(
            outgoing.reshape(devices, capacity, feature_dim),
            ("cent", "rows"),
            split_axis=0,
            concat_axis=0,
            tiled=True,
        ),
        lax.all_to_all(
            present.reshape(devices, capacity),
            ("cent", "rows"),
            split_axis=0,
            concat_axis=0,
            tiled=True,
        ),
    )
    members = received.reshape(devices * capacity, feature_dim)
    valid = arrived.reshape(devices * capacity) > 0.5
    scores, center = cluster_stats(members, valid)
    returned = lax.all_to_all(
        scores.reshape(devices, capacity), ("cent", "rows"), split_axis=0, concat_axis=0, tiled=True
    )
    dedup_score = returned.reshape(devices * capacity)[slot]
    return (perturbed_max, dedup_score, center[None, :])


def solution(mesh):
    in_specs = (
        P(("cent", "rows"), None),
        P(("cent", "rows"), None),
        P(("cent", "rows"), None),
        P(),
    )
    out_specs = (P(("cent", "rows")), P(("cent", "rows")), P(("cent", "rows"), None))
    return jax.shard_map(shards, mesh=mesh, in_specs=in_specs, out_specs=out_specs, check_vma=False)
```

profile of v0, /device:TPU:0, one launch (start us, length us, event | category | flops | bytes accessed | tf_op | source)
XLA Modules:
  0.0 242.6 jit_solution(4939791693935059020)
XLA Ops:
  10.3 2.2 scatter_custom_fusion
  13.2 11.1 %all-to-all-start = ((bf16[128,1,4]{2,1,0:T(2,128)(2,1)}), bf16[128,1,4]{2,1,0:T(2,128)(2,1)S(1)}, u32[]{:S(2)}, u32[]{:S(2)}) async-start(bf16[128,1,4]{2,1,0:T(2,128)(2,1)} %all_to_all.17), calls=%async_computation | async-start | bytes 131072 | tf_op jit(solution)/shard_map/all_to_all | solution.py:98
  24.3 3.5 %scatter_custom_fusion.1 = bf16[512,2048]{1,0:T(8,128)(2,1)S(1)} fusion(s32[256]{0:T(256)S(1)} %bitcast.32, bf16[256,2048]{1,0:T(8,128)(2,1)} %param.6, bf16[]{:T(256)} %constant.99.clone.1), kind=kCustom, calls=%fused_computation.50 | custom fusion | bytes 2097664 | tf_op jit(solution)/shard_map/scatter | solution.py:84
  27.9 2.2 reshape.113
  30.1 3.5 %all-to-all-done = bf16[128,1,4]{2,1,0:T(2,128)(2,1)S(1)} async-done(((bf16[128,1,4]{2,1,0:T(2,128)(2,1)}), bf16[128,1,4]{2,1,0:T(2,128)(2,1)S(1)}, u32[]{:S(2)}, u32[]{:S(2)}) %all-to-all-start) | async-done | bytes 1056 | tf_op jit(solution)/shard_map/all_to_all | solution.py:98
  33.6 6.3 %all-to-all-start.1 = ((bf16[128,4,2048]{2,1,0:T(4,128)(2,1)}), bf16[128,4,2048]{2,1,0:T(4,128)(2,1)S(1)}, u32[]{:S(2)}, u32[]{:S(2)}) async-start(bf16[128,4,2048]{2,1,0:T(4,128)(2,1)} %reshape.113), calls=%async_computation.1 | async-start | bytes 4194304 | tf_op jit(solution)/shard_map/all_to_all | solution.py:91
  40.7 32.1 %all-to-all-done.1 = bf16[128,4,2048]{2,1,0:T(4,128)(2,1)S(1)} async-done(((bf16[128,4,2048]{2,1,0:T(4,128)(2,1)}), bf16[128,4,2048]{2,1,0:T(4,128)(2,1)S(1)}, u32[]{:S(2)}, u32[]{:S(2)}) %all-to-all-start.1) | async-done | bytes 2097184 | tf_op jit(solution)/shard_map/all_to_all | solution.py:91
  72.8 2.1 fusion.33
  75.1 2.1 reshape.114
  77.1 3.6 %fusion.37 = f32[512]{0:T(512)S(1)} fusion(bf16[512,2048]{1,0:T(8,128)(2,1)} %reshape.114, f32[512]{0:T(512)S(1)} %rsqrt.18, pred[512]{0:T(512)(128)(4,1)S(1)} %gt.22), kind=kOutput, calls=%fused_computation.49 | convolution fusion | flops 1075576320 | bytes 2101760 | tf_op jit(solution)/shard_map/dot_general | solution.py:31
  81.5 7.2 %all-to-all-start.2 = ((f32[128,1,4]{2,1,0:T(1,128)}), f32[128,1,4]{2,1,0:T(1,128)S(1)}, u32[]{:S(2)}, u32[]{:S(2)}) async-start(f32[128,1,4]{2,1,0:T(1,128)} %bitcast.5), calls=%async_computation.2 | async-start | bytes 131072 | tf_op jit(solution)/shard_map/all_to_all | solution.py:109
  90.6 7.2 %all-to-all-done.2 = f32[128,1,4]{2,1,0:T(1,128)S(1)} async-done(((f32[128,1,4]{2,1,0:T(1,128)}), f32[128,1,4]{2,1,0:T(1,128)S(1)}, u32[]{:S(2)}, u32[]{:S(2)}) %all-to-all-start.2) | async-done | bytes 2080 | tf_op jit(solution)/shard_map/all_to_all | solution.py:109
  99.3 2.5 %gather_fusion = f32[256]{0:T(256)} fusion(f32[512]{0:T(512)S(1)} %reshape.115, s32[1024]{0:T(1024)S(1)} %pad_clamp_fusion), kind=kCustom, calls=%fused_computation | custom fusion | bytes 3072 | tf_op jit(solution)/shard_map/gather | solution.py:112
  101.8 57.1 %all-gather.3.cloned.1.call-done = bf16[4096,2048]{1,0:T(8,128)(2,1)} async-done(((bf16[128,2048]{1,0:T(8,128)(2,1)}), bf16[4096,2048]{1,0:T(8,128)(2,1)}) %all-gather.3.cloned.1.call-update) | async-done | bytes 16777232 | tf_op jit(solution)/shard_map/all_gather | solution.py:59
  158.8 65.8 %while.11 = (s32[]{:T(128)}, f32[1024]{0:T(1024)S(1)}, bf16[8,512,2048]{2,1,0:T(8,128)(2,1)}, bf16[1024,2048]{1,0:T(8,128)(2,1)}, s32[8]{0:T(128)S(1)}, /*index=...) while((s32[]{:T(128)}, f32[1024]{0:T(1024)S(1)}, bf16[8,512,2048]{2,1,0:T(8,128)(2,1)}, ...), condition=%wide.region_2.3_spmd.clone, body=%wide.region_0.2_spmd.clone.sunk | while | flops 2157464576 | bytes 6320795 | solution.py:76
  160.1 6.9 %fusion.56 = f32[1024]{0:T(1024)S(1)} fusion(bf16[1024,2048]{1,0:T(8,128)(2,1)} %get-tuple-element.168, bf16[8,512,2048]{2,1,0:T(8,128)(2,1)} %get-tuple-element.167, s32[]{:T(128)S(6)} %copy.19, s32[]{:T(128)} %get-tuple-element.171, s32[512]{0:T(512)S(1)} %add_multiply_fusion.2, s32[1024]{0:T(1024)S(1)} %fusion.55), kind=kOutput, calls=%fused_computation.21.clone.1 | convolution fusion | flops 2157444096 | bytes 6302212 | tf_op jit(solution)/shard_map/while/body/eval_jaxpr/dot_general | solution.py:67
  168.3 6.9 %fusion.56 = f32[1024]{0:T(1024)S(1)} fusion(bf16[1024,2048]{1,0:T(8,128)(2,1)} %get-tuple-element.168, bf16[8,512,2048]{2,1,0:T(8,128)(2,1)} %get-tuple-element.167, s32[]{:T(128)S(6)} %copy.19, s32[]{:T(128)} %get-tuple-element.171, s32[512]{0:T(512)S(1)} %add_multiply_fusion.2, s32[1024]{0:T(1024)S(1)} %fusion.55), kind=kOutput, calls=%fused_computation.21.clone.1 | convolution fusion | flops 2157444096 | bytes 6302212 | tf_op jit(solution)/shard_map/while/body/eval_jaxpr/dot_general | solution.py:67
  176.5 6.9 %fusion.56 = f32[1024]{0:T(1024)S(1)} fusion(bf16[1024,2048]{1,0:T(8,128)(2,1)} %get-tuple-element.168, bf16[8,512,2048]{2,1,0:T(8,128)(2,1)} %get-tuple-element.167, s32[]{:T(128)S(6)} %copy.19, s32[]{:T(128)} %get-tuple-element.171, s32[512]{0:T(512)S(1)} %add_multiply_fusion.2, s32[1024]{0:T(1024)S(1)} %fusion.55), kind=kOutput, calls=%fused_computation.21.clone.1 | convolution fusion | flops 2157444096 | bytes 6302212 | tf_op jit(solution)/shard_map/while/body/eval_jaxpr/dot_general | solution.py:67
  184.8 6.9 %fusion.56 = f32[1024]{0:T(1024)S(1)} fusion(bf16[1024,2048]{1,0:T(8,128)(2,1)} %get-tuple-element.168, bf16[8,512,2048]{2,1,0:T(8,128)(2,1)} %get-tuple-element.167, s32[]{:T(128)S(6)} %copy.19, s32[]{:T(128)} %get-tuple-element.171, s32[512]{0:T(512)S(1)} %add_multiply_fusion.2, s32[1024]{0:T(1024)S(1)} %fusion.55), kind=kOutput, calls=%fused_computation.21.clone.1 | convolution fusion | flops 2157444096 | bytes 6302212 | tf_op jit(solution)/shard_map/while/body/eval_jaxpr/dot_general | solution.py:67
  193.0 6.9 %fusion.56 = f32[1024]{0:T(1024)S(1)} fusion(bf16[1024,2048]{1,0:T(8,128)(2,1)} %get-tuple-element.168, bf16[8,512,2048]{2,1,0:T(8,128)(2,1)} %get-tuple-element.167, s32[]{:T(128)S(6)} %copy.19, s32[]{:T(128)} %get-tuple-element.171, s32[512]{0:T(512)S(1)} %add_multiply_fusion.2, s32[1024]{0:T(1024)S(1)} %fusion.55), kind=kOutput, calls=%fused_computation.21.clone.1 | convolution fusion | flops 2157444096 | bytes 6302212 | tf_op jit(solution)/shard_map/while/body/eval_jaxpr/dot_general | solution.py:67
  201.2 6.9 %fusion.56 = f32[1024]{0:T(1024)S(1)} fusion(bf16[1024,2048]{1,0:T(8,128)(2,1)} %get-tuple-element.168, bf16[8,512,2048]{2,1,0:T(8,128)(2,1)} %get-tuple-element.167, s32[]{:T(128)S(6)} %copy.19, s32[]{:T(128)} %get-tuple-element.171, s32[512]{0:T(512)S(1)} %add_multiply_fusion.2, s32[1024]{0:T(1024)S(1)} %fusion.55), kind=kOutput, calls=%fused_computation.21.clone.1 | convolution fusion | flops 2157444096 | bytes 6302212 | tf_op jit(solution)/shard_map/while/body/eval_jaxpr/dot_general | solution.py:67
  209.4 6.9 %fusion.56 = f32[1024]{0:T(1024)S(1)} fusion(bf16[1024,2048]{1,0:T(8,128)(2,1)} %get-tuple-element.168, bf16[8,512,2048]{2,1,0:T(8,128)(2,1)} %get-tuple-element.167, s32[]{:T(128)S(6)} %copy.19, s32[]{:T(128)} %get-tuple-element.171, s32[512]{0:T(512)S(1)} %add_multiply_fusion.2, s32[1024]{0:T(1024)S(1)} %fusion.55), kind=kOutput, calls=%fused_computation.21.clone.1 | convolution fusion | flops 2157444096 | bytes 6302212 | tf_op jit(solution)/shard_map/while/body/eval_jaxpr/dot_general | solution.py:67
  217.7 6.9 %fusion.56 = f32[1024]{0:T(1024)S(1)} fusion(bf16[1024,2048]{1,0:T(8,128)(2,1)} %get-tuple-element.168, bf16[8,512,2048]{2,1,0:T(8,128)(2,1)} %get-tuple-element.167, s32[]{:T(128)S(6)} %copy.19, s32[]{:T(128)} %get-tuple-element.171, s32[512]{0:T(512)S(1)} %add_multiply_fusion.2, s32[1024]{0:T(1024)S(1)} %fusion.55), kind=kOutput, calls=%fused_computation.21.clone.1 | convolution fusion | flops 2157444096 | bytes 6302212 | tf_op jit(solution)/shard_map/while/body/eval_jaxpr/dot_general | solution.py:67
  224.6 10.5 %pmax.7 = f32[1024]{0:T(1024)S(1)} all-reduce(f32[1024]{0:T(1024)S(1)} %get-tuple-element.45), channel_id=1, replica_groups=mesh['cent'=4,'rows'=32] {'cent'}, use_global_device_ids=true, to_apply=%region_3.4 | all-reduce | flops 1024 | bytes 8192 | tf_op jit(solution)/shard_map/pmax | solution.py:77
  (59 shorter events, 13.9 us)
Async XLA Ops:
  7.2 94.6 %all-gather.5.cloned.1.call-start = ((), (), s32[]{:S(2)}) async-start(), calls=%async_computation.4 | async-start | bytes 5242880 | tf_op jit(solution)/shard_map/all_gather | solution.py:54
  7.9 150.9 %all-gather.3.cloned.1.call-start = ((), (), s32[]{:S(2)}) async-start(), calls=%async_computation.3 | async-start | bytes 17301504 | tf_op jit(solution)/shard_map/all_gather | solution.py:59
  13.2 20.4 %all-to-all-start = ((bf16[128,1,4]{2,1,0:T(2,128)(2,1)}), bf16[128,1,4]{2,1,0:T(2,128)(2,1)S(1)}, u32[]{:S(2)}, u32[]{:S(2)}) async-start(bf16[128,1,4]{2,1,0:T(2,128)(2,1)} %all_to_all.17), calls=%async_computation | async-start | bytes 131072 | tf_op jit(solution)/shard_map/all_to_all | solution.py:98
  33.6 39.2 %all-to-all-start.1 = ((bf16[128,4,2048]{2,1,0:T(4,128)(2,1)}), bf16[128,4,2048]{2,1,0:T(4,128)(2,1)S(1)}, u32[]{:S(2)}, u32[]{:S(2)}) async-start(bf16[128,4,2048]{2,1,0:T(4,128)(2,1)} %reshape.113), calls=%async_computation.1 | async-start | bytes 4194304 | tf_op jit(solution)/shard_map/all_to_all | solution.py:91
  81.5 16.3 %all-to-all-start.2 = ((f32[128,1,4]{2,1,0:T(1,128)}), f32[128,1,4]{2,1,0:T(1,128)S(1)}, u32[]{:S(2)}, u32[]{:S(2)}) async-start(f32[128,1,4]{2,1,0:T(1,128)} %bitcast.5), calls=%async_computation.2 | async-start | bytes 131072 | tf_op jit(solution)/shard_map/all_to_all | solution.py:109
Sparse Core Ops, SparseCore 0:
  9.7 73.9 all-gather.4
  85.9 72.9 all-gather.2
where the time goes:
time: 243 us
  waiting for transfers between devices  101 us (42%)
  matrix products  59 us (24%)
  starting transfers between devices  24.7 us (10%)
  local copies, waits for them, and re-layouts  20.6 us (8%)
  between operations  14.9 us (6%)
  blocking collectives  10.5 us (4%)
  other arithmetic  6.36 us (3%)
  loops' own time  5.28 us (2%)
    all_gather x1, waiting for transfers between devices, shards(): piece = lax.all_gather(centroids, 'rows', axis=0, tiled=True)  57.1 us
    dot_general x8, matrix products, step(): lax.dot_general(group, tile, (((1,), (1,)), ((), ())), preferred_element_...  55.4 us
    all_to_all x1, waiting for transfers between devices, shards(): lax.all_to_all(outgoing.reshape(devices, capacity, feature_dim), ('cent',...  32.1 us
    all_to_all x1, starting transfers between devices, shards(): lax.all_to_all(present.reshape(devices, capacity), ('cent', 'rows'), spli...  11.1 us
    pmax x1, blocking collectives, shards(): merged = lax.pmax(result, 'cent')  10.5 us
    all_to_all x1, waiting for transfers between devices, shards(): lax.all_to_all(scores.reshape(devices, capacity), ('cent', 'rows'), split...  7.23 us
    all_to_all x1, starting transfers between devices, shards(): lax.all_to_all(scores.reshape(devices, capacity), ('cent', 'rows'), split...  7.22 us
    all_to_all x1, starting transfers between devices, shards(): lax.all_to_all(outgoing.reshape(devices, capacity, feature_dim), ('cent',...  6.27 us
  transfers between devices with their start and end apart: 5, of which 4 were waited for; matrix products, arithmetic and copies ran while one was open for 10% of the time, Pallas kernels for 0%

commit v1 on v0

--- a/solution.py
+++ b/solution.py
@@ -56,7 +56,14 @@
     group_ids = (position // rows_dev * rows_count + rows_index) * rows_dev + position % rows_dev
     panel_base = cent_index * (rows_count * cent_dev)
     initial = jnp.full((cent_count * rows_dev,), -1e30, jnp.float32)
-    piece = lax.all_gather(centroids, "rows", axis=0, tiled=True)
+
+    def _keep_up_columns(load):
+        buffer = []
+        for _ in range(lax.axis_size("rows")):
+            buffer.append(load)
+        return jnp.concatenate(lax.all_to_all(jnp.stack(buffer, 0), "rows", 0, 0), 0)
+
+    piece = _keep_up_columns(centroids)
     piece_rows = piece.shape[0]
     block = math.gcd(piece_rows, 512)
     tiles = piece.reshape(piece_rows // block, block, feature_dim)

time: 243 us -> 397 us (1.63)
  waiting for transfers between devices: 101 us -> 240 us
  blocking collectives: 10.5 us -> 22.4 us
  local copies, waits for them, and re-layouts: 20.6 us -> 25.7 us
    all_to_all x1, waiting for transfers between devices: 7.23 us -> 163 us  [_keep_up_columns(): lax.all_to_all(jnp.stack(buffer, 0), 'rows', 0, 0)]
    all_gather x1 -> x0, waiting for transfers between devices: 57.1 us -> none  [shards(): piece = lax.all_gather(centroids, 'rows', axis=0, tiled=True)]
    all_gather x1, waiting for transfers between devices: 0.01 us -> 43.7 us  [shards(): group = lax.all_gather(embeddings, 'cent', axis=0, tiled=True)]
    all_to_all x0 -> x1, blocking collectives: none -> 13.6 us  [shards(): lax.all_to_all(scores.reshape(devices, capacity), ('cent', 'rows'), split...]
    another operation x0 -> x1, local copies, waits for them, and re-layouts: none -> 5.94 us  [_keep_up_columns(): jnp.stack(buffer, 0)]
  transfers between devices with their start and end apart: 5 -> 4, of which waited for: 4 -> 4; matrix products, arithmetic and copies ran while one was open for 10% -> 3% of each run, Pallas kernels for 0% -> 0%
where the time goes in v1:
time: 397 us; the launch traced here: 396 us
  waiting for transfers between devices  240 us (60%)
  matrix products  59.1 us (15%)
  local copies, waits for them, and re-layouts  25.7 us (6%)
  starting transfers between devices  22.7 us (6%)
  blocking collectives  22.4 us (6%)
  between operations  14.9 us (4%)
  other arithmetic  6.35 us (2%)
  loops' own time  4.89 us (1%)
    all_to_all x1, waiting for transfers between devices, _keep_up_columns(): lax.all_to_all(jnp.stack(buffer, 0), 'rows', 0, 0)  163 us
    dot_general x8, matrix products, step(): lax.dot_general(group, tile, (((1,), (1,)), ((), ())), preferred_element_...  55.4 us
    all_gather x1, waiting for transfers between devices, shards(): group = lax.all_gather(embeddings, 'cent', axis=0, tiled=True)  43.7 us
    all_to_all x1, waiting for transfers between devices, shards(): lax.all_to_all(outgoing.reshape(devices, capacity, feature_dim), ('cent',...  29.6 us
    all_to_all x1, blocking collectives, shards(): lax.all_to_all(scores.reshape(devices, capacity), ('cent', 'rows'), split...  13.6 us
    all_to_all x1, starting transfers between devices, shards(): lax.all_to_all(present.reshape(devices, capacity), ('cent', 'rows'), spli...  11.1 us
    pmax x1, blocking collectives, shards(): merged = lax.pmax(result, 'cent')  8.8 us
  transfers between devices with their start and end apart: 4, of which 4 were waited for; matrix products, arithmetic and copies ran while one was open for 3% of the time, Pallas kernels for 0%

profile of v1, /device:TPU:0, one launch (start us, length us, event | category | flops | bytes accessed | tf_op | source)
XLA Modules:
  0.0 396.3 jit_solution(1367589415131992252)
XLA Ops:
  8.8 2.2 scatter_custom_fusion
  11.7 11.1 %all-to-all-start.1 = ((bf16[128,1,4]{2,1,0:T(2,128)(2,1)}), bf16[128,1,4]{2,1,0:T(2,128)(2,1)S(1)}, u32[]{:S(2)}, u32[]{:S(2)}) async-start(bf16[128,1,4]{2,1,0:T(2,128)(2,1)} %all_to_all.21), calls=%async_computation.1 | async-start | bytes 131072 | tf_op jit(solution)/shard_map/all_to_all | solution.py:105
  22.9 3.5 scatter_custom_fusion.1
  26.4 2.2 reshape.111
  28.6 3.6 all-to-all-done.1
  32.2 6.2 %all-to-all-start.2 = ((bf16[128,4,2048]{2,1,0:T(4,128)(2,1)}), bf16[128,4,2048]{2,1,0:T(4,128)(2,1)S(1)}, u32[]{:S(2)}, u32[]{:S(2)}) async-start(bf16[128,4,2048]{2,1,0:T(4,128)(2,1)} %reshape.111), calls=%async_computation.2 | async-start | bytes 4194304 | tf_op jit(solution)/shard_map/all_to_all | solution.py:98
  39.2 29.6 %all-to-all-done.2 = bf16[128,4,2048]{2,1,0:T(4,128)(2,1)S(1)} async-done(((bf16[128,4,2048]{2,1,0:T(4,128)(2,1)}), bf16[128,4,2048]{2,1,0:T(4,128)(2,1)S(1)}, u32[]{:S(2)}, u32[]{:S(2)}) %all-to-all-start.2) | async-done | bytes 2097184 | tf_op jit(solution)/shard_map/all_to_all | solution.py:98
  73.1 3.7 fusion.37
  76.9 13.6 %all_to_all.26 = f32[128,1,4]{2,1,0:T(1,128)S(1)} all-to-all(f32[128,1,4]{2,1,0:T(1,128)S(1)} %bitcast.29), channel_id=1, replica_groups=mesh['cent'=4,'rows'=32] {'cent','rows'}, dimensions={0} | all-to-all | bytes 4096 | tf_op jit(solution)/shard_map/all_to_all | solution.py:116
  90.5 5.9 %stack.2 = bf16[32,128,2048]{2,1,0:T(8,128)(2,1)} broadcast(bf16[128,2048]{1,0:T(8,128)(2,1)S(1)} %copy-done), dimensions={1,2} | broadcast | bytes 17301504 | tf_op jit(solution)/shard_map/stack | solution.py:64
  96.5 5.2 %all-to-all-start = ((bf16[32,128,2048]{2,1,0:T(8,128)(2,1)}), bf16[32,128,2048]{2,1,0:T(8,128)(2,1)}, u32[]{:S(2)}, u32[]{:S(2)}) async-start(bf16[32,128,2048]{2,1,0:T(8,128)(2,1)} %stack.2), calls=%async_computation | async-start | bytes 33554432 | tf_op jit(solution)/shard_map/all_to_all | solution.py:64
  105.7 2.5 gather_fusion
  108.2 43.7 %all-gather.2.cloned.1.call-done = bf16[1024,2048]{1,0:T(8,128)(2,1)} async-done(((bf16[256,2048]{1,0:T(8,128)(2,1)}), bf16[1024,2048]{1,0:T(8,128)(2,1)}) %all-gather.2.cloned.1.call-update) | async-done | bytes 4194320 | tf_op jit(solution)/shard_map/all_gather | solution.py:54
  151.9 162.9 %all-to-all-done = bf16[32,128,2048]{2,1,0:T(8,128)(2,1)} async-done(((bf16[32,128,2048]{2,1,0:T(8,128)(2,1)}), bf16[32,128,2048]{2,1,0:T(8,128)(2,1)}, u32[]{:S(2)}, u32[]{:S(2)}) %all-to-all-start) | async-done | bytes 16777248 | tf_op jit(solution)/shard_map/all_to_all | solution.py:64
  314.9 65.1 %while.11 = (s32[]{:T(128)}, f32[1024]{0:T(1024)S(1)}, bf16[8,512,2048]{2,1,0:T(8,128)(2,1)}, bf16[1024,2048]{1,0:T(8,128)(2,1)}, s32[8]{0:T(128)S(1)}, /*index=...) while((s32[]{:T(128)}, f32[1024]{0:T(1024)S(1)}, bf16[8,512,2048]{2,1,0:T(8,128)(2,1)}, ...), condition=%wide.region_2.3_spmd.clone, body=%wide.region_0.2_spmd.clone.sunk | while | flops 2157464576 | bytes 6320795 | solution.py:83
  316.0 6.9 %fusion.56 = f32[1024]{0:T(1024)S(1)} fusion(bf16[1024,2048]{1,0:T(8,128)(2,1)} %get-tuple-element.168, bf16[8,512,2048]{2,1,0:T(8,128)(2,1)} %get-tuple-element.167, s32[]{:T(128)S(6)} %copy.19, s32[]{:T(128)} %get-tuple-element.171, s32[512]{0:T(512)S(1)} %add_multiply_fusion.2, s32[1024]{0:T(1024)S(1)} %fusion.55), kind=kOutput, calls=%fused_computation.21.clone.1 | convolution fusion | flops 2157444096 | bytes 6302212 | tf_op jit(solution)/shard_map/while/body/eval_jaxpr/dot_general | solution.py:74
  324.2 6.9 %fusion.56 = f32[1024]{0:T(1024)S(1)} fusion(bf16[1024,2048]{1,0:T(8,128)(2,1)} %get-tuple-element.168, bf16[8,512,2048]{2,1,0:T(8,128)(2,1)} %get-tuple-element.167, s32[]{:T(128)S(6)} %copy.19, s32[]{:T(128)} %get-tuple-element.171, s32[512]{0:T(512)S(1)} %add_multiply_fusion.2, s32[1024]{0:T(1024)S(1)} %fusion.55), kind=kOutput, calls=%fused_computation.21.clone.1 | convolution fusion | flops 2157444096 | bytes 6302212 | tf_op jit(solution)/shard_map/while/body/eval_jaxpr/dot_general | solution.py:74
  332.3 6.9 %fusion.56 = f32[1024]{0:T(1024)S(1)} fusion(bf16[1024,2048]{1,0:T(8,128)(2,1)} %get-tuple-element.168, bf16[8,512,2048]{2,1,0:T(8,128)(2,1)} %get-tuple-element.167, s32[]{:T(128)S(6)} %copy.19, s32[]{:T(128)} %get-tuple-element.171, s32[512]{0:T(512)S(1)} %add_multiply_fusion.2, s32[1024]{0:T(1024)S(1)} %fusion.55), kind=kOutput, calls=%fused_computation.21.clone.1 | convolution fusion | flops 2157444096 | bytes 6302212 | tf_op jit(solution)/shard_map/while/body/eval_jaxpr/dot_general | solution.py:74
  340.5 6.9 %fusion.56 = f32[1024]{0:T(1024)S(1)} fusion(bf16[1024,2048]{1,0:T(8,128)(2,1)} %get-tuple-element.168, bf16[8,512,2048]{2,1,0:T(8,128)(2,1)} %get-tuple-element.167, s32[]{:T(128)S(6)} %copy.19, s32[]{:T(128)} %get-tuple-element.171, s32[512]{0:T(512)S(1)} %add_multiply_fusion.2, s32[1024]{0:T(1024)S(1)} %fusion.55), kind=kOutput, calls=%fused_computation.21.clone.1 | convolution fusion | flops 2157444096 | bytes 6302212 | tf_op jit(solution)/shard_map/while/body/eval_jaxpr/dot_general | solution.py:74
  348.6 6.9 %fusion.56 = f32[1024]{0:T(1024)S(1)} fusion(bf16[1024,2048]{1,0:T(8,128)(2,1)} %get-tuple-element.168, bf16[8,512,2048]{2,1,0:T(8,128)(2,1)} %get-tuple-element.167, s32[]{:T(128)S(6)} %copy.19, s32[]{:T(128)} %get-tuple-element.171, s32[512]{0:T(512)S(1)} %add_multiply_fusion.2, s32[1024]{0:T(1024)S(1)} %fusion.55), kind=kOutput, calls=%fused_computation.21.clone.1 | convolution fusion | flops 2157444096 | bytes 6302212 | tf_op jit(solution)/shard_map/while/body/eval_jaxpr/dot_general | solution.py:74
  356.8 6.9 %fusion.56 = f32[1024]{0:T(1024)S(1)} fusion(bf16[1024,2048]{1,0:T(8,128)(2,1)} %get-tuple-element.168, bf16[8,512,2048]{2,1,0:T(8,128)(2,1)} %get-tuple-element.167, s32[]{:T(128)S(6)} %copy.19, s32[]{:T(128)} %get-tuple-element.171, s32[512]{0:T(512)S(1)} %add_multiply_fusion.2, s32[1024]{0:T(1024)S(1)} %fusion.55), kind=kOutput, calls=%fused_computation.21.clone.1 | convolution fusion | flops 2157444096 | bytes 6302212 | tf_op jit(solution)/shard_map/while/body/eval_jaxpr/dot_general | solution.py:74
  364.9 6.9 %fusion.56 = f32[1024]{0:T(1024)S(1)} fusion(bf16[1024,2048]{1,0:T(8,128)(2,1)} %get-tuple-element.168, bf16[8,512,2048]{2,1,0:T(8,128)(2,1)} %get-tuple-element.167, s32[]{:T(128)S(6)} %copy.19, s32[]{:T(128)} %get-tuple-element.171, s32[512]{0:T(512)S(1)} %add_multiply_fusion.2, s32[1024]{0:T(1024)S(1)} %fusion.55), kind=kOutput, calls=%fused_computation.21.clone.1 | convolution fusion | flops 2157444096 | bytes 6302212 | tf_op jit(solution)/shard_map/while/body/eval_jaxpr/dot_general | solution.py:74
  373.0 6.9 %fusion.56 = f32[1024]{0:T(1024)S(1)} fusion(bf16[1024,2048]{1,0:T(8,128)(2,1)} %get-tuple-element.168, bf16[8,512,2048]{2,1,0:T(8,128)(2,1)} %get-tuple-element.167, s32[]{:T(128)S(6)} %copy.19, s32[]{:T(128)} %get-tuple-element.171, s32[512]{0:T(512)S(1)} %add_multiply_fusion.2, s32[1024]{0:T(1024)S(1)} %fusion.55), kind=kOutput, calls=%fused_computation.21.clone.1 | convolution fusion | flops 2157444096 | bytes 6302212 | tf_op jit(solution)/shard_map/while/body/eval_jaxpr/dot_general | solution.py:74
  380.0 8.8 %pmax.7 = f32[1024]{0:T(1024)S(1)} all-reduce(f32[1024]{0:T(1024)S(1)} %get-tuple-element.45), channel_id=1, replica_groups=mesh['cent'=4,'rows'=32] {'cent'}, use_global_device_ids=true, to_apply=%region_3.4 | all-reduce | flops 1024 | bytes 8192 | tf_op jit(solution)/shard_map/pmax | solution.py:84
  (60 shorter events, 16.4 us)
Async XLA Ops:
  11.7 20.4 %all-to-all-start.1 = ((bf16[128,1,4]{2,1,0:T(2,128)(2,1)}), bf16[128,1,4]{2,1,0:T(2,128)(2,1)S(1)}, u32[]{:S(2)}, u32[]{:S(2)}) async-start(bf16[128,1,4]{2,1,0:T(2,128)(2,1)} %all_to_all.21), calls=%async_computation.1 | async-start | bytes 131072 | tf_op jit(solution)/shard_map/all_to_all | solution.py:105
  32.2 36.6 %all-to-all-start.2 = ((bf16[128,4,2048]{2,1,0:T(4,128)(2,1)}), bf16[128,4,2048]{2,1,0:T(4,128)(2,1)S(1)}, u32[]{:S(2)}, u32[]{:S(2)}) async-start(bf16[128,4,2048]{2,1,0:T(4,128)(2,1)} %reshape.111), calls=%async_computation.2 | async-start | bytes 4194304 | tf_op jit(solution)/shard_map/all_to_all | solution.py:98
  73.1 17.4 %copy-start = (bf16[128,2048]{1,0:T(8,128)(2,1)S(1)}, bf16[128,2048]{1,0:T(8,128)(2,1)}, u32[]{:S(2)}) copy-start(bf16[128,2048]{1,0:T(8,128)(2,1)} %param.7) | copy-start | bytes 1572868
  96.5 218.4 %all-to-all-start = ((bf16[32,128,2048]{2,1,0:T(8,128)(2,1)}), bf16[32,128,2048]{2,1,0:T(8,128)(2,1)}, u32[]{:S(2)}, u32[]{:S(2)}) async-start(bf16[32,128,2048]{2,1,0:T(8,128)(2,1)} %stack.2), calls=%async_computation | async-start | bytes 33554432 | tf_op jit(solution)/shard_map/all_to_all | solution.py:64
  101.6 50.3 %all-gather.2.cloned.1.call-start = ((), (), s32[]{:S(2)}) async-start(), calls=%async_computation.4 | async-start | bytes 5242880 | tf_op jit(solution)/shard_map/all_gather | solution.py:54
Sparse Core Ops, SparseCore 0:
  104.1 47.7 all-gather.1
